TPU v7x, 32 devices: a whole 2x2x4 slice. The times are simulated.
32 devices in a mesh: fsdp: 2 (over x), ctx: 4 (over y, core), tp: 4 (over z).
Axes of the slice: x: 2, y: 2, z: 4, core: 2. Of those that a mesh axis runs over, the one named last changes fastest.
Arguments:
- tokens: bfloat16 [2048, 4, 1024], P(('ctx', 'tp'), 'fsdp'), may hold values from -6 to 6
- segment_ids: int32 [4, 2048], P('fsdp', 'ctx'), may hold values from 0 to 5, never falling along the last dimension, each value on 1 to 800 neighbouring positions
- decay_rate: float32 [8], P('tp'), may hold values from 0.0005 to 0.07
- w_query: float32 [1024, 1024], P(('fsdp', 'ctx'), 'tp'), may hold values from -0.1875 to 0.1875
- w_key: float32 [1024, 1024], P(('fsdp', 'ctx'), 'tp'), may hold values from -0.1875 to 0.1875
- w_value: float32 [1024, 1024], P(('fsdp', 'ctx'), 'tp'), may hold values from -0.1875 to 0.1875
- w_gate: float32 [1024, 1024], P(('fsdp', 'ctx'), 'tp'), may hold values from -0.1875 to 0.1875
- w_out: float32 [1024, 1024], P('tp', ('fsdp', 'ctx')), may hold values from -0.375 to 0.375
- glu_left: float32 [1024, 2816], P(('fsdp', 'ctx'), 'tp'), may hold values from -0.1875 to 0.1875
- glu_right: float32 [1024, 2816], P(('fsdp', 'ctx'), 'tp'), may hold values from -0.1875 to 0.1875
- glu_down: float32 [2816, 1024], P('tp', ('fsdp', 'ctx')), may hold values from -0.109375 to 0.109375
- cotangent: bfloat16 [2048, 4, 1024], P(('ctx', 'tp'), 'fsdp'), may hold values from -6 to 6
Outputs:
- output: bfloat16 [2048, 4, 1024], P(('ctx', 'tp'), 'fsdp')
- grad_tokens: float32 [2048, 4, 1024], P(('ctx', 'tp'), 'fsdp')
- grad_query: float32 [1024, 1024], P(('fsdp', 'ctx'), 'tp')
- grad_key: float32 [1024, 1024], P(('fsdp', 'ctx'), 'tp')
- grad_value: float32 [1024, 1024], P(('fsdp', 'ctx'), 'tp')
- grad_gate: float32 [1024, 1024], P(('fsdp', 'ctx'), 'tp')
- grad_out: float32 [1024, 1024], P('tp', ('fsdp', 'ctx'))
- grad_left: float32 [1024, 2816], P(('fsdp', 'ctx'), 'tp')
- grad_right: float32 [1024, 2816], P(('fsdp', 'ctx'), 'tp')
- grad_down: float32 [2816, 1024], P('tp', ('fsdp', 'ctx'))
Inputs may be any that keep to these rules, and one draw needn't show every extreme that they name: `segment_ids`: along each sequence the document numbers never fall; every document has 1 to 800 tokens and one has exactly 800.
All inputs are finite; a program needn't handle non-finite values.
Results may differ from a plain program's by a relative error of at most 0.013.
Values may be sent and summed in bfloat16 or wider, within the bound.
A program may use at most 128 MiB of HBM per device.

v0:
```python
import jax
import jax.numpy as jnp
from jax import lax
from jax.sharding import PartitionSpec as P

DH = 128
EPSILON = 1e-06
HEAD_FLOOR = 1.0
HIGHEST = lax.Precision.HIGHEST


def entering(x, axis, join, neutral):
    place = lax.axis_index(axis)
    gathered = jax.tree.map(
        lambda a, kind: lax.all_gather(a.astype(kind), axis),
        x,
        (jnp.bfloat16, jnp.bfloat16, jnp.bfloat16, jnp.bfloat16),
    )
    state = jax.tree.map(lambda a, e: jnp.zeros_like(a) + jnp.asarray(e, a.dtype), x, neutral)

    def one(lap, state):
        return join(
            state,
            jax.tree.map(
                lambda a, own: lax.dynamic_index_in_dim(a, lap, 0, False).astype(own.dtype),
                gathered,
                x,
            ),
        )

    return lax.fori_loop(0, place, one, state)


def entering_2(x, axis, join, neutral):
    count = lax.axis_size(axis)
    place = lax.axis_index(axis)
    ahead = count - 1 - place
    gathered = jax.tree.map(
        lambda a, kind: lax.all_gather(a.astype(kind), axis), x, (jnp.bfloat16, jnp.bfloat16)
    )
    state = jax.tree.map(lambda a, e: jnp.zeros_like(a) + jnp.asarray(e, a.dtype), x, neutral)

    def one(lap, state):
        source = count - 1 - lap
        return join(
            state,
            jax.tree.map(
                lambda a, own: lax.dynamic_index_in_dim(a, source, 0, False).astype(own.dtype),
                gathered,
                x,
            ),
        )

    return lax.fori_loop(0, ahead, one, state)


def normalize(values, floor_value=EPSILON):
    return values * lax.rsqrt(jnp.mean(values * values, axis=-1, keepdims=True) + floor_value)


def norm_backward(values, upstream, floor_value=EPSILON):
    inverse = lax.rsqrt(jnp.mean(values * values, axis=-1, keepdims=True) + floor_value)
    inner_mean = jnp.mean(upstream * values, axis=-1, keepdims=True)
    return inverse * (upstream - values * inner_mean * inverse * inverse)


def silu_slope(values):
    sigmoid_value = jax.nn.sigmoid(values)
    return sigmoid_value * (1.0 + values * (1.0 - sigmoid_value))


def chain_forward(earlier, later):
    early_first, early_last, early_decay, early_state = earlier
    late_first, late_last, late_decay, late_state = later
    linked = (late_first == early_last) | (early_last < 0.0) | (late_first < 0.0)
    carried = jnp.where(linked[:, None], late_decay, 0.0)
    first_seg = jnp.where(early_first < 0.0, late_first, early_first)
    last_seg = jnp.where(late_last < 0.0, early_last, late_last)
    return (
        first_seg,
        last_seg,
        early_decay * carried,
        late_state + carried[:, :, None, None] * early_state,
    )


def chain_backward(earlier, later):
    return (earlier[0] * later[0], later[1] + later[0][:, :, None, None] * earlier[1])


def shards(
    tokens,
    segment_ids,
    decay_rate,
    w_query,
    w_key,
    w_value,
    w_gate,
    w_out,
    glu_left,
    glu_right,
    glu_down,
    cotangent,
):
    shard_len, seq_count, model_width = tokens.shape
    tok_float = tokens.astype(jnp.float32)
    normed_part = normalize(tok_float).astype(jnp.bfloat16)
    gathered = (
        lax.all_gather(w_query.astype(jnp.bfloat16), ("fsdp", "ctx"), axis=0, tiled=True),
        lax.all_gather(w_key.astype(jnp.bfloat16), ("fsdp", "ctx"), axis=0, tiled=True),
        lax.all_gather(w_value.astype(jnp.bfloat16), ("fsdp", "ctx"), axis=0, tiled=True),
        lax.all_gather(w_gate.astype(jnp.bfloat16), ("fsdp", "ctx"), axis=0, tiled=True),
        lax.all_gather(w_out.astype(jnp.bfloat16), ("fsdp", "ctx"), axis=1, tiled=True),
        lax.all_gather(glu_left.astype(jnp.bfloat16), ("fsdp", "ctx"), axis=0, tiled=True),
        lax.all_gather(glu_right.astype(jnp.bfloat16), ("fsdp", "ctx"), axis=0, tiled=True),
        lax.all_gather(glu_down.astype(jnp.bfloat16), ("fsdp", "ctx"), axis=1, tiled=True),
    )
    full_query, full_key, full_value, full_gate, full_out, full_left, full_right, full_down = (
        gathered
    )
    normed = lax.all_gather(normed_part, "tp", axis=0, tiled=True)
    block_len = normed.shape[0]
    total_rows = block_len * seq_count
    normed_flat = normed.reshape(total_rows, model_width)
    local_width = full_query.shape[1]
    head_count = local_width // DH
    head_shape = (block_len, seq_count, head_count, DH)
    proj_query = jnp.dot(normed_flat, full_query, preferred_element_type=jnp.float32)
    proj_key = jnp.dot(normed_flat, full_key, preferred_element_type=jnp.float32)
    proj_value = jnp.dot(normed_flat, full_value, preferred_element_type=jnp.float32)
    proj_gate = jnp.dot(normed_flat, full_gate, preferred_element_type=jnp.float32)
    queries = jax.nn.silu(proj_query).astype(jnp.bfloat16).reshape(head_shape)
    keys_low = jax.nn.silu(proj_key).astype(jnp.bfloat16).reshape(head_shape)
    values_low = proj_value.astype(jnp.bfloat16).reshape(head_shape)
    seg_pos = segment_ids.T
    seg_float = seg_pos.astype(jnp.float32)
    position = jnp.arange(block_len).astype(jnp.float32)
    distance = position[:, None] - position[None, :]
    same_doc = (segment_ids[:, :, None] == segment_ids[:, None, :]) & (distance >= 0.0)[None]
    decay_grid = jnp.where(
        same_doc[:, None],
        jnp.exp(-decay_rate[None, :, None, None] * jnp.maximum(distance, 0.0)[None, None]),
        0.0,
    )
    end_weight = jnp.where(
        (seg_pos == seg_pos[-1:])[:, :, None],
        jnp.exp(-(block_len - 1.0 - position)[:, None, None] * decay_rate[None, None, :]),
        0.0,
    )
    keys_end = (keys_low.astype(jnp.float32) * end_weight[..., None]).astype(jnp.bfloat16)
    update = jnp.einsum("tbhd,tbhe->bhde", keys_end, values_low, preferred_element_type=jnp.float32)
    first_seg = seg_float[0]
    last_seg = seg_float[-1]
    span_decay = jnp.where(
        (first_seg == last_seg)[:, None], jnp.exp(-block_len * decay_rate)[None, :], 0.0
    )
    identity = (
        -jnp.ones((seq_count,), jnp.float32),
        -jnp.ones((seq_count,), jnp.float32),
        jnp.ones((seq_count, head_count), jnp.float32),
        jnp.zeros((seq_count, head_count, DH, DH), jnp.float32),
    )
    scanned = entering((first_seg, last_seg, span_decay, update), "ctx", chain_forward, identity)
    prior_last = scanned[1]
    state_low = scanned[3].astype(jnp.bfloat16)
    inflow = jnp.where(
        (seg_pos == prior_last[None, :])[:, :, None],
        jnp.exp(-(position + 1.0)[:, None, None] * decay_rate[None, None, :]),
        0.0,
    )
    scores = jnp.einsum("tbhd,sbhd->bhts", queries, keys_low, preferred_element_type=jnp.float32)
    weights_low = (scores * decay_grid).astype(jnp.bfloat16)
    intra = jnp.einsum(
        "bhts,sbhd->tbhd", weights_low, values_low, preferred_element_type=jnp.float32
    )
    inter = (
        jnp.einsum("tbhd,bhde->tbhe", queries, state_low, preferred_element_type=jnp.float32)
        * inflow[..., None]
    )
    attended = intra + inter
    attended_norm = normalize(attended, HEAD_FLOOR)
    gate_value = jax.nn.sigmoid(proj_gate).reshape(head_shape)
    mixed_heads = (
        (attended_norm * gate_value).astype(jnp.bfloat16).reshape(block_len, seq_count, local_width)
    )
    row_count = shard_len * lax.axis_size("tp")
    piece_rows = mixed_heads.reshape(row_count * seq_count, local_width)
    branch = lax.psum_scatter(
        jnp.dot(piece_rows, full_out, preferred_element_type=jnp.float32).reshape(
            row_count, seq_count, model_width
        ),
        "tp",
        scatter_dimension=0,
        tiled=True,
    )
    residual = tok_float + branch
    second_part = normalize(residual).astype(jnp.bfloat16)
    second = lax.all_gather(second_part, "tp", axis=0, tiled=True)
    second_flat = second.reshape(total_rows, model_width)
    left_proj = jnp.dot(second_flat, full_left, preferred_element_type=jnp.float32)
    right_proj = jnp.dot(second_flat, full_right, preferred_element_type=jnp.float32)
    hidden = (left_proj * right_proj).astype(jnp.bfloat16)
    ffn_width = hidden.shape[1]
    hidden_blocks = hidden.reshape(block_len, seq_count, ffn_width)
    row_count = shard_len * lax.axis_size("tp")
    piece_rows = hidden_blocks.reshape(row_count * seq_count, ffn_width)
    ffn_branch = lax.psum_scatter(
        jnp.dot(piece_rows, full_down, preferred_element_type=jnp.float32)
        .reshape(row_count, seq_count, model_width)
        .astype(jnp.bfloat16),
        "tp",
        scatter_dimension=0,
        tiled=True,
    ).astype(jnp.float32)
    output = (residual + ffn_branch).astype(jnp.bfloat16)
    upstream = lax.all_gather(cotangent, "tp", axis=0, tiled=True).reshape(total_rows, model_width)
    grad_down = jnp.dot(hidden.T, upstream, preferred_element_type=jnp.float32)
    grad_hidden = jnp.dot(upstream, full_down.T, preferred_element_type=jnp.float32)
    grad_left_proj = (grad_hidden * right_proj).astype(jnp.bfloat16)
    grad_right_proj = (grad_hidden * left_proj).astype(jnp.bfloat16)
    grad_left = jnp.dot(second_flat.T, grad_left_proj, preferred_element_type=jnp.float32)
    grad_right = jnp.dot(second_flat.T, grad_right_proj, preferred_element_type=jnp.float32)
    left_blocks = grad_left_proj.reshape(block_len, seq_count, ffn_width)
    right_blocks = grad_right_proj.reshape(block_len, seq_count, ffn_width)
    row_count = shard_len * lax.axis_size("tp")
    left_rows = left_blocks.reshape(row_count * seq_count, ffn_width)
    right_rows = right_blocks.reshape(row_count * seq_count, ffn_width)
    summed = jnp.dot(left_rows, full_left.T, preferred_element_type=jnp.float32) + jnp.dot(
        right_rows, full_right.T, preferred_element_type=jnp.float32
    )
    grad_second = lax.psum_scatter(
        summed.reshape(row_count, seq_count, model_width), "tp", scatter_dimension=0, tiled=True
    )
    grad_residual = cotangent.astype(jnp.float32) + norm_backward(residual, grad_second)
    branch_low = grad_residual.astype(jnp.bfloat16)
    grad_branch = lax.all_gather(branch_low, "tp", axis=0, tiled=True).reshape(
        total_rows, model_width
    )
    grad_wout = jnp.dot(
        mixed_heads.reshape(total_rows, local_width).T,
        grad_branch,
        preferred_element_type=jnp.float32,
    )
    grad_mixed = jnp.dot(grad_branch, full_out.T, preferred_element_type=jnp.float32).reshape(
        head_shape
    )
    grad_gate_proj = (
        (grad_mixed * attended_norm * gate_value * (1.0 - gate_value))
        .astype(jnp.bfloat16)
        .reshape(total_rows, local_width)
    )
    grad_attended = norm_backward(attended, grad_mixed * gate_value, HEAD_FLOOR).astype(
        jnp.bfloat16
    )
    grad_weights = jnp.einsum(
        "tbhd,sbhd->bhts", grad_attended, values_low, preferred_element_type=jnp.float32
    )
    grad_scores = (grad_weights * decay_grid).astype(jnp.bfloat16)
    grad_queries = jnp.einsum(
        "bhts,sbhd->tbhd", grad_scores, keys_low, preferred_element_type=jnp.float32
    )
    grad_queries = (
        grad_queries
        + jnp.einsum(
            "tbhe,bhde->tbhd", grad_attended, state_low, preferred_element_type=jnp.float32
        )
        * inflow[..., None]
    )
    grad_keys = jnp.einsum(
        "bhts,tbhd->sbhd", grad_scores, queries, preferred_element_type=jnp.float32
    )
    grad_values = jnp.einsum(
        "bhts,tbhd->sbhd", weights_low, grad_attended, preferred_element_type=jnp.float32
    )
    weighted_queries = queries.astype(jnp.float32) * inflow[..., None]
    grad_prior_local = jnp.einsum(
        "tbhd,tbhe->bhde", weighted_queries, grad_attended.astype(jnp.float32), precision=HIGHEST
    )
    link_decay = jnp.where((first_seg == prior_last)[:, None], span_decay, 0.0)
    back_identity = (
        jnp.ones((seq_count, head_count), jnp.float32),
        jnp.zeros((seq_count, head_count, DH, DH), jnp.float32),
    )
    grad_update = entering_2((link_decay, grad_prior_local), "ctx", chain_backward, back_identity)[
        1
    ]
    grad_values = grad_values + jnp.einsum(
        "tbhd,bhde->tbhe", keys_end.astype(jnp.float32), grad_update, precision=HIGHEST
    )
    grad_keys = (
        grad_keys
        + jnp.einsum(
            "tbhe,bhde->tbhd", values_low.astype(jnp.float32), grad_update, precision=HIGHEST
        )
        * end_weight[..., None]
    )
    grad_query_proj = (
        (grad_queries * silu_slope(proj_query).reshape(head_shape))
        .astype(jnp.bfloat16)
        .reshape(total_rows, local_width)
    )
    grad_key_proj = (
        (grad_keys * silu_slope(proj_key).reshape(head_shape))
        .astype(jnp.bfloat16)
        .reshape(total_rows, local_width)
    )
    grad_value_proj = grad_values.astype(jnp.bfloat16).reshape(total_rows, local_width)
    grad_wquery = jnp.dot(normed_flat.T, grad_query_proj, preferred_element_type=jnp.float32)
    grad_wkey = jnp.dot(normed_flat.T, grad_key_proj, preferred_element_type=jnp.float32)
    grad_wvalue = jnp.dot(normed_flat.T, grad_value_proj, preferred_element_type=jnp.float32)
    grad_wgate = jnp.dot(normed_flat.T, grad_gate_proj, preferred_element_type=jnp.float32)
    query_blocks = grad_query_proj.reshape(block_len, seq_count, local_width)
    key_blocks = grad_key_proj.reshape(block_len, seq_count, local_width)
    value_blocks = grad_value_proj.reshape(block_len, seq_count, local_width)
    gate_blocks = grad_gate_proj.reshape(block_len, seq_count, local_width)
    row_count = shard_len * lax.axis_size("tp")
    summed = jnp.zeros((row_count * seq_count, model_width), jnp.float32)
    for grad_blocks, weight_full in (
        (query_blocks, full_query),
        (key_blocks, full_key),
        (value_blocks, full_value),
        (gate_blocks, full_gate),
    ):
        piece_rows = grad_blocks.reshape(row_count * seq_count, local_width)
        summed = summed + jnp.dot(piece_rows, weight_full.T, preferred_element_type=jnp.float32)
    grad_normed = lax.psum_scatter(
        summed.reshape(row_count, seq_count, model_width).astype(jnp.bfloat16),
        "tp",
        scatter_dimension=0,
        tiled=True,
    ).astype(jnp.float32)
    grad_tokens = grad_residual + norm_backward(tok_float, grad_normed)
    every_grad = (
        lax.psum_scatter(grad_wquery, ("fsdp", "ctx"), scatter_dimension=0, tiled=True),
        lax.psum_scatter(grad_wkey, ("fsdp", "ctx"), scatter_dimension=0, tiled=True),
        lax.psum_scatter(grad_wvalue, ("fsdp", "ctx"), scatter_dimension=0, tiled=True),
        lax.psum_scatter(grad_wgate, ("fsdp", "ctx"), scatter_dimension=0, tiled=True),
        lax.psum_scatter(grad_wout, ("fsdp", "ctx"), scatter_dimension=1, tiled=True),
        lax.psum_scatter(grad_left, ("fsdp", "ctx"), scatter_dimension=0, tiled=True),
        lax.psum_scatter(grad_right, ("fsdp", "ctx"), scatter_dimension=0, tiled=True),
        lax.psum_scatter(grad_down, ("fsdp", "ctx"), scatter_dimension=1, tiled=True),
    )
    return (
        output,
        grad_tokens,
        every_grad[0],
        every_grad[1],
        every_grad[2],
        every_grad[3],
        every_grad[4],
        every_grad[5],
        every_grad[6],
        every_grad[7],
    )


def solution(mesh):
    in_specs = (
        P(("ctx", "tp"), "fsdp", None),
        P("fsdp", "ctx"),
        P("tp"),
        P(("fsdp", "ctx"), "tp"),
        P(("fsdp", "ctx"), "tp"),
        P(("fsdp", "ctx"), "tp"),
        P(("fsdp", "ctx"), "tp"),
        P("tp", ("fsdp", "ctx")),
        P(("fsdp", "ctx"), "tp"),
        P(("fsdp", "ctx"), "tp"),
        P("tp", ("fsdp", "ctx")),
        P(("ctx", "tp"), "fsdp", None),
    )
    out_specs = (
        P(("ctx", "tp"), "fsdp", None),
        P(("ctx", "tp"), "fsdp", None),
        P(("fsdp", "ctx"), "tp"),
        P(("fsdp", "ctx"), "tp"),
        P(("fsdp", "ctx"), "tp"),
        P(("fsdp", "ctx"), "tp"),
        P("tp", ("fsdp", "ctx")),
        P(("fsdp", "ctx"), "tp"),
        P(("fsdp", "ctx"), "tp"),
        P("tp", ("fsdp", "ctx")),
    )
    return jax.shard_map(shards, mesh=mesh, in_specs=in_specs, out_specs=out_specs, check_vma=False)
```

profile of v0, /device:TPU:0, one launch (start us, length us, event | category | flops | bytes accessed | tf_op | source)
XLA Modules:
  0.0 1034.6 jit_solution(431356184398698397)
XLA Ops:
  11.0 6.0 all-gather.3
  17.2 5.3 all-gather.2
  28.1 10.1 all_gather.67
  38.2 9.8 all_gather.65
  48.0 9.9 all_gather.66
  57.9 10.7 %all_gather.73 = bf16[1024,256]{1,0:T(8,128)(2,1)} all-gather(bf16[128,256]{1,0:T(8,128)(2,1)S(1)} %convert_element_type.256), channel_id=1, replica_groups=mesh['fsdp'=2,'ctx'=4,'tp'=4] {'fsdp','ctx'}, dimensions={0}, use_global_device_ids=true | all-gather | bytes 589824 | tf_op jit(solution)/shard_map/all_gather | solution.py:112
  68.7 10.1 all_gather.74
  102.0 7.8 all-gather
  134.3 80.6 %reduce-scatter.13.cloned.1.call-done = f32[128,2,1024]{2,0,1:T(8,128)} async-done(((f32[512,2,1024]{2,0,1:T(8,128)}), f32[128,2,1024]{2,0,1:T(8,128)}) %reduce-scatter.13.cloned.1.call-update) | async-done | bytes 1048592 | tf_op jit(solution)/shard_map/reduce_scatter | solution.py:188
  221.8 41.2 %all-gather.22.cloned.1.call-done = bf16[512,2,1024]{2,1,0:T(2,128)(2,1)} async-done(((bf16[128,2,1024]{2,1,0:T(2,128)(2,1)}), bf16[512,2,1024]{2,1,0:T(2,128)(2,1)}) %all-gather.22.cloned.1.call-update) | async-done | bytes 2097168 | tf_op jit(solution)/shard_map/all_gather | solution.py:216
  267.1 42.1 %all-gather.14.cloned.1.call-done = bf16[512,2,1024]{2,0,1:T(8,128)(2,1)} async-done(((bf16[128,2,1024]{2,0,1:T(8,128)(2,1)}), bf16[512,2,1024]{2,0,1:T(8,128)(2,1)}) %all-gather.14.cloned.1.call-update) | async-done | bytes 2097168 | tf_op jit(solution)/shard_map/all_gather | solution.py:198
  318.5 17.2 %all-gather.16.cloned.1.call-done = bf16[1024,704]{0,1:T(8,128)(2,1)} async-done(((bf16[128,704]{0,1:T(8,128)(2,1)}), bf16[1024,704]{0,1:T(8,128)(2,1)}) %all-gather.16.cloned.1.call-update) | async-done | bytes 1441808 | tf_op jit(solution)/shard_map/all_gather | solution.py:114
  335.7 5.3 fusion.68
  341.0 22.5 %all-gather.18.cloned.1.call-done = bf16[1024,704]{0,1:T(8,128)(2,1)} async-done(((bf16[128,704]{0,1:T(8,128)(2,1)}), bf16[1024,704]{0,1:T(8,128)(2,1)}) %all-gather.18.cloned.1.call-update) | async-done | bytes 1441808 | tf_op jit(solution)/shard_map/all_gather | solution.py:115
  363.5 5.2 fusion.69
  368.7 22.7 %all-gather.20.cloned.1.call-done = bf16[704,1024]{1,0:T(8,128)(2,1)} async-done(((bf16[704,128]{1,0:T(8,128)(2,1)}), bf16[704,1024]{1,0:T(8,128)(2,1)}) %all-gather.20.cloned.1.call-update) | async-done | bytes 1441808 | tf_op jit(solution)/shard_map/all_gather | solution.py:116
  391.4 6.8 multiply_convert_fusion
  404.5 6.0 reshape.426
  410.5 5.5 copy.115
  416.1 76.9 %reduce-scatter.17.cloned.1.call-done = f32[128,2,1024]{2,0,1:T(8,128)} async-done(((f32[512,2,1024]{2,0,1:T(8,128)}), f32[128,2,1024]{2,0,1:T(8,128)}) %reduce-scatter.17.cloned.1.call-update) | async-done | bytes 1048592 | tf_op jit(solution)/shard_map/reduce_scatter | solution.py:231
  511.6 31.4 %all-gather.24.cloned.1.call-done = bf16[512,2,1024]{2,0,1:T(8,128)(2,1)} async-done(((bf16[128,2,1024]{2,0,1:T(8,128)(2,1)}), bf16[512,2,1024]{2,0,1:T(8,128)(2,1)}) %all-gather.24.cloned.1.call-update) | async-done | bytes 2097168 | tf_op jit(solution)/shard_map/all_gather | solution.py:236
  554.6 7.3 all-gather.1
  582.1 5.6 add_convert_fusion
  648.5 33.1 %reduce-scatter.15.cloned.1.call-done = bf16[128,2,1024]{2,0,1:T(8,128)(2,1)} async-done(((bf16[512,2,1024]{2,0,1:T(8,128)(2,1)}), bf16[128,2,1024]{2,0,1:T(8,128)(2,1)}) %reduce-scatter.15.cloned.1.call-update) | async-done | bytes 524304 | tf_op jit(solution)/shard_map/reduce_scatter | solution.py:207
  686.6 43.0 %reduce-scatter.31.cloned.1.call-done = f32[128,704]{0,1:T(8,128)} async-done(((f32[1024,704]{0,1:T(8,128)}), f32[128,704]{0,1:T(8,128)}) %reduce-scatter.31.cloned.1.call-update) | async-done | bytes 360464 | tf_op jit(solution)/shard_map/reduce_scatter | solution.py:339
  729.6 49.2 %reduce-scatter.33.cloned.1.call-done = f32[128,704]{0,1:T(8,128)} async-done(((f32[1024,704]{0,1:T(8,128)}), f32[128,704]{0,1:T(8,128)}) %reduce-scatter.33.cloned.1.call-update) | async-done | bytes 360464 | tf_op jit(solution)/shard_map/reduce_scatter | solution.py:340
  778.9 48.7 %reduce-scatter.35.cloned.1.call-done = f32[704,128]{1,0:T(8,128)} async-done(((f32[704,1024]{1,0:T(8,128)}), f32[704,128]{1,0:T(8,128)}) %reduce-scatter.35.cloned.1.call-update) | async-done | bytes 360464 | tf_op jit(solution)/shard_map/reduce_scatter | solution.py:341
  827.6 40.0 %reduce-scatter.29.cloned.1.call-done = f32[256,128]{1,0:T(8,128)} async-done(((f32[256,1024]{1,0:T(8,128)}), f32[256,128]{1,0:T(8,128)}) %reduce-scatter.29.cloned.1.call-update) | async-done | bytes 131088 | tf_op jit(solution)/shard_map/reduce_scatter | solution.py:338
  867.6 40.0 %reduce-scatter.23.cloned.1.call-done = f32[128,256]{1,0:T(8,128)} async-done(((f32[1024,256]{1,0:T(8,128)}), f32[128,256]{1,0:T(8,128)}) %reduce-scatter.23.cloned.1.call-update) | async-done | bytes 131088 | tf_op jit(solution)/shard_map/reduce_scatter | solution.py:335
  907.6 40.0 %reduce-scatter.21.cloned.1.call-done = f32[128,256]{1,0:T(8,128)} async-done(((f32[1024,256]{1,0:T(8,128)}), f32[128,256]{1,0:T(8,128)}) %reduce-scatter.21.cloned.1.call-update) | async-done | bytes 131088 | tf_op jit(solution)/shard_map/reduce_scatter | solution.py:334
  947.6 40.0 %reduce-scatter.25.cloned.1.call-done = f32[128,256]{1,0:T(8,128)} async-done(((f32[1024,256]{1,0:T(8,128)}), f32[128,256]{1,0:T(8,128)}) %reduce-scatter.25.cloned.1.call-update) | async-done | bytes 131088 | tf_op jit(solution)/shard_map/reduce_scatter | solution.py:336
  987.5 40.1 %reduce-scatter.27.cloned.1.call-done = f32[128,256]{1,0:T(8,128)} async-done(((f32[1024,256]{1,0:T(8,128)}), f32[128,256]{1,0:T(8,128)}) %reduce-scatter.27.cloned.1.call-update) | async-done | bytes 131088 | tf_op jit(solution)/shard_map/reduce_scatter | solution.py:337
  (277 shorter events, 199.8 us)
Async XLA Ops:
  7.2 20.4 %copy-start.50 = (f32[128,256]{1,0:T(8,128)S(1)}, f32[128,256]{1,0:T(8,128)}, u32[]{:S(2)}) copy-start(f32[128,256]{1,0:T(8,128)} %param.21) | copy-start | bytes 393220
  7.2 20.6 %copy-start.51 = (f32[128,256]{1,0:T(8,128)S(1)}, f32[128,256]{1,0:T(8,128)}, u32[]{:S(2)}) copy-start(f32[128,256]{1,0:T(8,128)} %param.19) | copy-start | bytes 393220
  7.2 20.6 %copy-start.52 = (f32[128,256]{1,0:T(8,128)S(1)}, f32[128,256]{1,0:T(8,128)}, u32[]{:S(2)}) copy-start(f32[128,256]{1,0:T(8,128)} %param.22) | copy-start | bytes 393220
  7.2 20.6 %copy-start.53 = (f32[256,128]{1,0:T(8,128)S(1)}, f32[256,128]{1,0:T(8,128)}, u32[]{:S(2)}) copy-start(f32[256,128]{1,0:T(8,128)} %param.23) | copy-start | bytes 393220
  7.2 73.8 %all-gather.12.cloned.1.call-start = ((), (), s32[]{:S(2)}) async-start(), calls=%async_computation.12 | async-start | bytes 2621440 | tf_op jit(solution)/shard_map/all_gather | solution.py:121
  10.7 204.1 %reduce-scatter.13.cloned.1.call-start = ((), (), s32[]{:S(2)}) async-start(), calls=%async_computation.13 | async-start | bytes 5242880 | tf_op jit(solution)/shard_map/reduce_scatter | solution.py:188
  38.2 52.1 %copy-start.38 = (bf16[1024,256]{1,0:T(8,128)(2,1)}, bf16[1024,256]{1,0:T(8,128)(2,1)S(1)}, u32[]{:S(2)}) copy-start(bf16[1024,256]{1,0:T(8,128)(2,1)S(1)} %all_gather.67) | copy-start | bytes 1572868
  48.0 49.2 %copy-start.36 = (bf16[1024,256]{1,0:T(8,128)(2,1)}, bf16[1024,256]{1,0:T(8,128)(2,1)S(1)}, u32[]{:S(2)}) copy-start(bf16[1024,256]{1,0:T(8,128)(2,1)S(1)} %all_gather.65) | copy-start | bytes 1572868
  133.5 81.4 %copy-start = (bf16[128,2,1024]{2,1,0:T(2,128)(2,1)S(1)}, bf16[128,2,1024]{2,1,0:T(2,128)(2,1)}, u32[]{:S(2)}) copy-start(bf16[128,2,1024]{2,1,0:T(2,128)(2,1)} %param.16) | copy-start | bytes 1572868
  133.5 129.5 %all-gather.22.cloned.1.call-start = ((), (), s32[]{:S(2)}) async-start(), calls=%async_computation.19 | async-start | bytes 2621440 | tf_op jit(solution)/shard_map/all_gather | solution.py:216
  134.2 83.3 %copy-start.48 = (f32[128,704]{0,1:T(8,128)S(1)}, f32[128,704]{0,1:T(8,128)}, u32[]{:S(2)}) copy-start(f32[128,704]{0,1:T(8,128)} %param.24) | copy-start | bytes 1081348
  134.2 175.0 %all-gather.14.cloned.1.call-start = ((), (), s32[]{:S(2)}) async-start(), calls=%async_computation.14 | async-start | bytes 2621440 | tf_op jit(solution)/shard_map/all_gather | solution.py:198
  217.4 118.3 %all-gather.16.cloned.1.call-start = ((), (), s32[]{:S(2)}) async-start(), calls=%async_computation.15 | async-start | bytes 1622016 | tf_op jit(solution)/shard_map/all_gather | solution.py:114
  218.2 145.3 %all-gather.18.cloned.1.call-start = ((), (), s32[]{:S(2)}) async-start(), calls=%async_computation.16 | async-start | bytes 1622016 | tf_op jit(solution)/shard_map/all_gather | solution.py:115
  220.0 171.5 %all-gather.20.cloned.1.call-start = ((), (), s32[]{:S(2)}) async-start(), calls=%async_computation.17 | async-start | bytes 1622016 | tf_op jit(solution)/shard_map/all_gather | solution.py:116
  221.7 271.2 %reduce-scatter.17.cloned.1.call-start = ((), (), s32[]{:S(2)}) async-start(), calls=%async_computation.20 | async-start | bytes 5242880 | tf_op jit(solution)/shard_map/reduce_scatter | solution.py:231
  416.0 78.9 %copy-start.19 = (bf16[128,2,1024]{2,1,0:T(2,128)(2,1)S(1)}, bf16[128,2,1024]{2,1,0:T(2,128)(2,1)}, u32[]{:S(2)}) copy-start(bf16[128,2,1024]{2,1,0:T(2,128)(2,1)} %param.27) | copy-start | bytes 1572868
  416.0 127.0 %all-gather.24.cloned.1.call-start = ((), (), s32[]{:S(2)}) async-start(), calls=%async_computation.21 | async-start | bytes 2621440 | tf_op jit(solution)/shard_map/all_gather | solution.py:236
  496.4 150.7 %reduce-scatter.19.cloned.1.call-start = ((), (), s32[]{:S(2)}) async-start(), calls=%async_computation.22 | async-start | bytes 2621440 | tf_op jit(solution)/shard_map/reduce_scatter | solution.py:326
  506.5 36.4 %copy-start.24 = (bf16[256,1024]{1,0:T(8,128)(2,1)S(1)}, bf16[256,1024]{1,0:T(8,128)(2,1)}, u32[]{:S(2)}) copy-start(bf16[256,1024]{1,0:T(8,128)(2,1)} %all_gather.74) | copy-start | bytes 1572868
  593.7 87.9 %reduce-scatter.15.cloned.1.call-start = ((), (), s32[]{:S(2)}) async-start(), calls=%async_computation.18 | async-start | bytes 2621440 | tf_op jit(solution)/shard_map/reduce_scatter | solution.py:207
  602.9 126.7 %reduce-scatter.31.cloned.1.call-start = ((), (), s32[]{:S(2)}) async-start(), calls=%async_computation.28 | async-start | bytes 3244032 | tf_op jit(solution)/shard_map/reduce_scatter | solution.py:339
  609.1 169.8 %reduce-scatter.33.cloned.1.call-start = ((), (), s32[]{:S(2)}) async-start(), calls=%async_computation.29 | async-start | bytes 3244032 | tf_op jit(solution)/shard_map/reduce_scatter | solution.py:340
  615.4 212.3 %reduce-scatter.35.cloned.1.call-start = ((), (), s32[]{:S(2)}) async-start(), calls=%async_computation.30 | async-start | bytes 3244032 | tf_op jit(solution)/shard_map/reduce_scatter | solution.py:341
  621.7 245.9 %reduce-scatter.29.cloned.1.call-start = ((), (), s32[]{:S(2)}) async-start(), calls=%async_computation.27 | async-start | bytes 1179648 | tf_op jit(solution)/shard_map/reduce_scatter | solution.py:338
  633.1 274.5 %reduce-scatter.23.cloned.1.call-start = ((), (), s32[]{:S(2)}) async-start(), calls=%async_computation.24 | async-start | bytes 1179648 | tf_op jit(solution)/shard_map/reduce_scatter | solution.py:335
  636.6 311.0 %reduce-scatter.21.cloned.1.call-start = ((), (), s32[]{:S(2)}) async-start(), calls=%async_computation.23 | async-start | bytes 1179648 | tf_op jit(solution)/shard_map/reduce_scatter | solution.py:334
  640.1 347.5 %reduce-scatter.25.cloned.1.call-start = ((), (), s32[]{:S(2)}) async-start(), calls=%async_computation.25 | async-start | bytes 1179648 | tf_op jit(solution)/shard_map/reduce_scatter | solution.py:336
  643.5 384.1 %reduce-scatter.27.cloned.1.call-start = ((), (), s32[]{:S(2)}) async-start(), calls=%async_computation.26 | async-start | bytes 1179648 | tf_op jit(solution)/shard_map/reduce_scatter | solution.py:337
  643.6 38.0 %copy-start.20 = (bf16[128,2,1024]{2,1,0:T(2,128)(2,1)S(1)}, bf16[128,2,1024]{2,1,0:T(2,128)(2,1)}, u32[]{:S(2)}) copy-start(bf16[128,2,1024]{2,1,0:T(2,128)(2,1)} %param.27) | copy-start | bytes 1572868
  647.0 34.6 %copy-start.3 = (f32[128,2,1024]{2,0,1:T(8,128)S(1)}, f32[128,2,1024]{2,0,1:T(8,128)}, u32[]{:S(2)}) copy-start(f32[128,2,1024]{2,0,1:T(8,128)} %reduce-scatter.13.cloned.1.call-done) | copy-start | bytes 3145732
  647.0 34.6 %copy-start.11 = (f32[128,2,1024]{2,0,1:T(8,128)S(1)}, f32[128,2,1024]{2,0,1:T(8,128)}, u32[]{:S(2)}) copy-start(f32[128,2,1024]{2,0,1:T(8,128)} %reduce-scatter.17.cloned.1.call-done) | copy-start | bytes 3145732
  (45 other events, 164.8 us)
Sparse Core Ops, SparseCore 0:
  10.8 48.6 all-gather.11
  133.6 81.2 reduce-scatter.12
  216.5 46.4 all-gather.21
  264.5 44.6 all-gather.13
  311.7 24.0 all-gather.15
  338.2 25.2 all-gather.17
  366.1 25.2 all-gather.19
  416.1 76.7 reduce-scatter.16
  496.5 46.4 all-gather.23
  593.8 42.1 reduce-scatter.18
  638.4 43.1 reduce-scatter.14
  685.4 44.1 reduce-scatter.30
  734.0 44.8 reduce-scatter.32
  782.7 44.8 reduce-scatter.34
  831.5 36.0 reduce-scatter.28
  871.5 36.0 reduce-scatter.22
  911.5 36.0 reduce-scatter.20
  951.5 35.9 reduce-scatter.24
  991.6 35.9 reduce-scatter.26
where the time goes:
time: 1040 us; the launch traced here: 1030 us
  waiting for transfers between devices  710 us (68%)
  matrix products  107 us (10%)
  local copies, waits for them, and re-layouts  92.6 us (9%)
  blocking collectives  87 us (8%)
  other arithmetic  21.5 us (2%)
  between operations  15.3 us (1%)
    reduce_scatter x1, waiting for transfers between devices, shards(): lax.psum_scatter(jnp.dot(piece_rows, full_out, preferred_element_type=jnp...  80.6 us
    reduce_scatter x1, waiting for transfers between devices, shards(): lax.psum_scatter(summed.reshape(row_count, seq_count, model_width), 'tp',...  76.9 us
    reduce_scatter x1, waiting for transfers between devices, shards(): lax.psum_scatter(grad_right, ('fsdp', 'ctx'), scatter_dimension=0, tiled=...  49.2 us
    reduce_scatter x1, waiting for transfers between devices, shards(): lax.psum_scatter(grad_down, ('fsdp', 'ctx'), scatter_dimension=1, tiled=T...  48.7 us
    reduce_scatter x1, waiting for transfers between devices, shards(): lax.psum_scatter(grad_left, ('fsdp', 'ctx'), scatter_dimension=0, tiled=T...  43 us
    all_gather x1, waiting for transfers between devices, shards(): second = lax.all_gather(second_part, 'tp', axis=0, tiled=True)  42.1 us
    all_gather x1, waiting for transfers between devices, shards(): lax.all_gather(cotangent, 'tp', axis=0, tiled=True)  41.2 us
    reduce_scatter x1, waiting for transfers between devices, shards(): lax.psum_scatter(grad_wgate, ('fsdp', 'ctx'), scatter_dimension=0, tiled=...  40.1 us
  transfers between devices with their start and end apart: 19, of which 17 were waited for; matrix products, arithmetic and copies ran while one was open for 9% of the time, Pallas kernels for 0%

commit v1 on v0

--- a/solution.py
+++ b/solution.py
@@ -7,6 +7,24 @@
 EPSILON = 1e-06
 HEAD_FLOOR = 1.0
 HIGHEST = lax.Precision.HIGHEST
+
+
+def gather_around(array, axis, dim):
+    ways, here, step = (lax.axis_size(axis), lax.axis_index(axis), array.shape[dim])
+    dims = [n * ways if d == dim else n for d, n in enumerate(array.shape)]
+    full = lax.dynamic_update_slice_in_dim(
+        jnp.zeros(dims, array.dtype), array, here * step, axis=dim
+    )
+    going_up = going_down = array
+    for far in range(1, ways // 2 + 1):
+        going_up = lax.ppermute(going_up, axis, [(d, (d + 1) % ways) for d in range(ways)])
+        full = lax.dynamic_update_slice_in_dim(full, going_up, (here - far) % ways * step, axis=dim)
+        if 2 * far < ways:
+            going_down = lax.ppermute(going_down, axis, [(d, (d - 1) % ways) for d in range(ways)])
+            full = lax.dynamic_update_slice_in_dim(
+                full, going_down, (here + far) % ways * step, axis=dim
+            )
+    return full
 
 
 def entering(x, axis, join, neutral):
@@ -113,7 +131,7 @@
         lax.all_gather(w_out.astype(jnp.bfloat16), ("fsdp", "ctx"), axis=1, tiled=True),
         lax.all_gather(glu_left.astype(jnp.bfloat16), ("fsdp", "ctx"), axis=0, tiled=True),
         lax.all_gather(glu_right.astype(jnp.bfloat16), ("fsdp", "ctx"), axis=0, tiled=True),
-        lax.all_gather(glu_down.astype(jnp.bfloat16), ("fsdp", "ctx"), axis=1, tiled=True),
+        gather_around(glu_down.astype(jnp.bfloat16), ("fsdp", "ctx"), 1),
     )
     full_query, full_key, full_value, full_gate, full_out, full_left, full_right, full_down = (
         gathered

time: 1040 us -> 1020 us (0.981)
  waiting for transfers between devices: 710 us -> 672 us
    all_gather x1, waiting for transfers between devices: 41.2 us -> 15.9 us  [shards(): lax.all_gather(cotangent, 'tp', axis=0, tiled=True)]
    all_gather x1 -> x0, waiting for transfers between devices: 22.7 us -> none  [shards(): lax.all_gather(glu_down.astype(jnp.bfloat16), ('fsdp', 'ctx'), axis=1, ti...]
    ppermute x0 -> x7, waiting for transfers between devices: none -> 10.6 us  [the longest x4 10.4 us: gather_around(): lax.ppermute(going_up, axis, [(d, (d + 1) % ways) for d in range(ways)])]
  transfers between devices with their start and end apart: 19 -> 25, of which waited for: 17 -> 21; matrix products, arithmetic and copies ran while one was open for 9% -> 10% of each run, Pallas kernels for 0% -> 0%
where the time goes in v1:
time: 1020 us; the launch traced here: 1010 us
  waiting for transfers between devices  672 us (66%)
  matrix products  107 us (10%)
  local copies, waits for them, and re-layouts  97.3 us (10%)
  blocking collectives  87.4 us (9%)
  other arithmetic  23.5 us (2%)
  between operations  15.6 us (2%)
    reduce_scatter x1, waiting for transfers between devices, shards(): lax.psum_scatter(jnp.dot(piece_rows, full_out, preferred_element_type=jnp...  80.6 us
    reduce_scatter x1, waiting for transfers between devices, shards(): lax.psum_scatter(summed.reshape(row_count, seq_count, model_width), 'tp',...  76.9 us
    reduce_scatter x1, waiting for transfers between devices, shards(): lax.psum_scatter(grad_right, ('fsdp', 'ctx'), scatter_dimension=0, tiled=...  49.1 us
    reduce_scatter x1, waiting for transfers between devices, shards(): lax.psum_scatter(grad_down, ('fsdp', 'ctx'), scatter_dimension=1, tiled=T...  48.9 us
    reduce_scatter x1, waiting for transfers between devices, shards(): lax.psum_scatter(grad_left, ('fsdp', 'ctx'), scatter_dimension=0, tiled=T...  43.2 us
    all_gather x1, waiting for transfers between devices, shards(): second = lax.all_gather(second_part, 'tp', axis=0, tiled=True)  42.1 us
    reduce_scatter x1, waiting for transfers between devices, shards(): lax.psum_scatter(grad_wgate, ('fsdp', 'ctx'), scatter_dimension=0, tiled=...  40 us
    reduce_scatter x1, waiting for transfers between devices, shards(): lax.psum_scatter(grad_wquery, ('fsdp', 'ctx'), scatter_dimension=0, tiled...  40 us
  transfers between devices with their start and end apart: 25, of which 21 were waited for; matrix products, arithmetic and copies ran while one was open for 10% of the time, Pallas kernels for 0%

profile of v1, /device:TPU:0, one launch (start us, length us, event | category | flops | bytes accessed | tf_op | source)
XLA Modules:
  0.0 1013.4 jit_solution(14438286218828970677)
XLA Ops:
  11.0 6.0 all-gather.3
  17.2 5.3 all-gather.2
  28.1 10.1 all_gather.64
  38.2 9.8 all_gather.62
  48.0 9.9 all_gather.63
  57.9 10.7 %all_gather.70 = bf16[1024,256]{1,0:T(8,128)(2,1)} all-gather(bf16[128,256]{1,0:T(8,128)(2,1)S(1)} %convert_element_type.256), channel_id=1, replica_groups=mesh['fsdp'=2,'ctx'=4,'tp'=4] {'fsdp','ctx'}, dimensions={0}, use_global_device_ids=true | all-gather | bytes 589824 | tf_op jit(solution)/shard_map/all_gather | solution.py:130
  68.7 10.1 all_gather.71
  81.0 5.1 copy.98
  102.0 7.8 all-gather
  133.4 80.6 %reduce-scatter.13.cloned.1.call-done = f32[128,2,1024]{2,0,1:T(8,128)} async-done(((f32[512,2,1024]{2,0,1:T(8,128)}), f32[128,2,1024]{2,0,1:T(8,128)}) %reduce-scatter.13.cloned.1.call-update) | async-done | bytes 1048592 | tf_op jit(solution)/shard_map/reduce_scatter | solution.py:206
  246.2 15.9 %all-gather.19.cloned.1.call-done = bf16[512,2,1024]{2,1,0:T(2,128)(2,1)} async-done(((bf16[128,2,1024]{2,1,0:T(2,128)(2,1)}), bf16[512,2,1024]{2,1,0:T(2,128)(2,1)}) %all-gather.19.cloned.1.call-update) | async-done | bytes 2097168 | tf_op jit(solution)/shard_map/all_gather | solution.py:234
  266.2 42.1 %all-gather.13.cloned.1.call-done = bf16[512,2,1024]{2,0,1:T(8,128)(2,1)} async-done(((bf16[128,2,1024]{2,0,1:T(8,128)(2,1)}), bf16[512,2,1024]{2,0,1:T(8,128)(2,1)}) %all-gather.13.cloned.1.call-update) | async-done | bytes 2097168 | tf_op jit(solution)/shard_map/all_gather | solution.py:216
  308.3 5.1 copy.112
  317.6 17.3 %all-gather.15.cloned.1.call-done = bf16[1024,704]{0,1:T(8,128)(2,1)} async-done(((bf16[128,704]{0,1:T(8,128)(2,1)}), bf16[1024,704]{0,1:T(8,128)(2,1)}) %all-gather.15.cloned.1.call-update) | async-done | bytes 1441808 | tf_op jit(solution)/shard_map/all_gather | solution.py:132
  334.8 5.2 fusion.70
  340.0 22.6 %all-gather.17.cloned.1.call-done = bf16[1024,704]{0,1:T(8,128)(2,1)} async-done(((bf16[128,704]{0,1:T(8,128)(2,1)}), bf16[1024,704]{0,1:T(8,128)(2,1)}) %all-gather.17.cloned.1.call-update) | async-done | bytes 1441808 | tf_op jit(solution)/shard_map/all_gather | solution.py:133
  377.4 6.0 reshape.426
  383.4 5.5 copy.115
  389.0 76.9 %reduce-scatter.17.cloned.1.call-done = f32[128,2,1024]{2,0,1:T(8,128)} async-done(((f32[512,2,1024]{2,0,1:T(8,128)}), f32[128,2,1024]{2,0,1:T(8,128)}) %reduce-scatter.17.cloned.1.call-update) | async-done | bytes 1048592 | tf_op jit(solution)/shard_map/reduce_scatter | solution.py:249
  469.5 5.0 all_gather.79
  484.7 31.3 %all-gather.21.cloned.1.call-done = bf16[512,2,1024]{2,0,1:T(8,128)(2,1)} async-done(((bf16[128,2,1024]{2,0,1:T(8,128)(2,1)}), bf16[512,2,1024]{2,0,1:T(8,128)(2,1)}) %all-gather.21.cloned.1.call-update) | async-done | bytes 2097168 | tf_op jit(solution)/shard_map/all_gather | solution.py:254
  527.7 7.7 all-gather.1
  561.4 5.6 add_convert_fusion
  627.3 32.7 %reduce-scatter.15.cloned.1.call-done = bf16[128,2,1024]{2,0,1:T(8,128)(2,1)} async-done(((bf16[512,2,1024]{2,0,1:T(8,128)(2,1)}), bf16[128,2,1024]{2,0,1:T(8,128)(2,1)}) %reduce-scatter.15.cloned.1.call-update) | async-done | bytes 524304 | tf_op jit(solution)/shard_map/reduce_scatter | solution.py:225
  665.1 43.2 %reduce-scatter.31.cloned.1.call-done = f32[128,704]{0,1:T(8,128)} async-done(((f32[1024,704]{0,1:T(8,128)}), f32[128,704]{0,1:T(8,128)}) %reduce-scatter.31.cloned.1.call-update) | async-done | bytes 360464 | tf_op jit(solution)/shard_map/reduce_scatter | solution.py:357
  708.2 49.1 %reduce-scatter.33.cloned.1.call-done = f32[128,704]{0,1:T(8,128)} async-done(((f32[1024,704]{0,1:T(8,128)}), f32[128,704]{0,1:T(8,128)}) %reduce-scatter.33.cloned.1.call-update) | async-done | bytes 360464 | tf_op jit(solution)/shard_map/reduce_scatter | solution.py:358
  757.3 48.9 %reduce-scatter.35.cloned.1.call-done = f32[704,128]{1,0:T(8,128)} async-done(((f32[704,1024]{1,0:T(8,128)}), f32[704,128]{1,0:T(8,128)}) %reduce-scatter.35.cloned.1.call-update) | async-done | bytes 360464 | tf_op jit(solution)/shard_map/reduce_scatter | solution.py:359
  806.2 40.0 %reduce-scatter.29.cloned.1.call-done = f32[256,128]{1,0:T(8,128)} async-done(((f32[256,1024]{1,0:T(8,128)}), f32[256,128]{1,0:T(8,128)}) %reduce-scatter.29.cloned.1.call-update) | async-done | bytes 131088 | tf_op jit(solution)/shard_map/reduce_scatter | solution.py:356
  846.2 40.0 %reduce-scatter.23.cloned.1.call-done = f32[128,256]{1,0:T(8,128)} async-done(((f32[1024,256]{1,0:T(8,128)}), f32[128,256]{1,0:T(8,128)}) %reduce-scatter.23.cloned.1.call-update) | async-done | bytes 131088 | tf_op jit(solution)/shard_map/reduce_scatter | solution.py:353
  886.2 40.0 %reduce-scatter.21.cloned.1.call-done = f32[128,256]{1,0:T(8,128)} async-done(((f32[1024,256]{1,0:T(8,128)}), f32[128,256]{1,0:T(8,128)}) %reduce-scatter.21.cloned.1.call-update) | async-done | bytes 131088 | tf_op jit(solution)/shard_map/reduce_scatter | solution.py:352
  926.2 40.0 %reduce-scatter.25.cloned.1.call-done = f32[128,256]{1,0:T(8,128)} async-done(((f32[1024,256]{1,0:T(8,128)}), f32[128,256]{1,0:T(8,128)}) %reduce-scatter.25.cloned.1.call-update) | async-done | bytes 131088 | tf_op jit(solution)/shard_map/reduce_scatter | solution.py:354
  966.1 40.0 %reduce-scatter.27.cloned.1.call-done = f32[128,256]{1,0:T(8,128)} async-done(((f32[1024,256]{1,0:T(8,128)}), f32[128,256]{1,0:T(8,128)}) %reduce-scatter.27.cloned.1.call-update) | async-done | bytes 131088 | tf_op jit(solution)/shard_map/reduce_scatter | solution.py:355
  (302 shorter events, 225.6 us)
Async XLA Ops:
  7.2 73.7 %all-gather.11.cloned.1.call-start = ((), (), s32[]{:S(2)}) async-start(), calls=%async_computation.12 | async-start | bytes 2621440 | tf_op jit(solution)/shard_map/all_gather | solution.py:139
  10.7 203.3 %reduce-scatter.13.cloned.1.call-start = ((), (), s32[]{:S(2)}) async-start(), calls=%async_computation.13 | async-start | bytes 5242880 | tf_op jit(solution)/shard_map/reduce_scatter | solution.py:206
  38.2 52.0 %copy-start.36 = (bf16[1024,256]{1,0:T(8,128)(2,1)}, bf16[1024,256]{1,0:T(8,128)(2,1)S(1)}, u32[]{:S(2)}) copy-start(bf16[1024,256]{1,0:T(8,128)(2,1)S(1)} %all_gather.64) | copy-start | bytes 1572868
  48.0 49.2 %copy-start.35 = (bf16[1024,256]{1,0:T(8,128)(2,1)}, bf16[1024,256]{1,0:T(8,128)(2,1)S(1)}, u32[]{:S(2)}) copy-start(bf16[1024,256]{1,0:T(8,128)(2,1)S(1)} %all_gather.62) | copy-start | bytes 1572868
  132.6 81.4 %copy-start = (bf16[128,2,1024]{2,1,0:T(2,128)(2,1)S(1)}, bf16[128,2,1024]{2,1,0:T(2,128)(2,1)}, u32[]{:S(2)}) copy-start(bf16[128,2,1024]{2,1,0:T(2,128)(2,1)} %param.16) | copy-start | bytes 1572868
  132.6 129.5 %all-gather.19.cloned.1.call-start = ((), (), s32[]{:S(2)}) async-start(), calls=%async_computation.18 | async-start | bytes 2621440 | tf_op jit(solution)/shard_map/all_gather | solution.py:234
  133.3 83.4 %copy-start.50 = (f32[128,704]{0,1:T(8,128)S(1)}, f32[128,704]{0,1:T(8,128)}, u32[]{:S(2)}) copy-start(f32[128,704]{0,1:T(8,128)} %param.24) | copy-start | bytes 1081348
  133.3 175.0 %all-gather.13.cloned.1.call-start = ((), (), s32[]{:S(2)}) async-start(), calls=%async_computation.14 | async-start | bytes 2621440 | tf_op jit(solution)/shard_map/all_gather | solution.py:216
  216.6 118.2 %all-gather.15.cloned.1.call-start = ((), (), s32[]{:S(2)}) async-start(), calls=%async_computation.15 | async-start | bytes 1622016 | tf_op jit(solution)/shard_map/all_gather | solution.py:132
  217.4 145.2 %all-gather.17.cloned.1.call-start = ((), (), s32[]{:S(2)}) async-start(), calls=%async_computation.16 | async-start | bytes 1622016 | tf_op jit(solution)/shard_map/all_gather | solution.py:133
  219.2 246.7 %reduce-scatter.17.cloned.1.call-start = ((), (), s32[]{:S(2)}) async-start(), calls=%async_computation.19 | async-start | bytes 5242880 | tf_op jit(solution)/shard_map/reduce_scatter | solution.py:249
  221.4 6.1 collective-permute-start
  221.4 6.1 collective-permute-start.1
  227.5 5.9 collective-permute-start.2
  227.5 6.0 collective-permute-start.3
  233.4 5.9 collective-permute-start.4
  233.6 6.8 collective-permute-start.5
  239.3 6.2 collective-permute-start.6
  389.0 78.9 %copy-start.21 = (bf16[128,2,1024]{2,1,0:T(2,128)(2,1)S(1)}, bf16[128,2,1024]{2,1,0:T(2,128)(2,1)}, u32[]{:S(2)}) copy-start(bf16[128,2,1024]{2,1,0:T(2,128)(2,1)} %param.27) | copy-start | bytes 1572868
  389.0 127.0 %all-gather.21.cloned.1.call-start = ((), (), s32[]{:S(2)}) async-start(), calls=%async_computation.20 | async-start | bytes 2621440 | tf_op jit(solution)/shard_map/all_gather | solution.py:254
  469.4 156.5 %reduce-scatter.19.cloned.1.call-start = ((), (), s32[]{:S(2)}) async-start(), calls=%async_computation.21 | async-start | bytes 2621440 | tf_op jit(solution)/shard_map/reduce_scatter | solution.py:344
  479.6 36.4 %copy-start.26 = (bf16[256,1024]{1,0:T(8,128)(2,1)S(1)}, bf16[256,1024]{1,0:T(8,128)(2,1)}, u32[]{:S(2)}) copy-start(bf16[256,1024]{1,0:T(8,128)(2,1)} %all_gather.71) | copy-start | bytes 1572868
  572.8 87.3 %reduce-scatter.15.cloned.1.call-start = ((), (), s32[]{:S(2)}) async-start(), calls=%async_computation.17 | async-start | bytes 2621440 | tf_op jit(solution)/shard_map/reduce_scatter | solution.py:225
  583.4 124.9 %reduce-scatter.31.cloned.1.call-start = ((), (), s32[]{:S(2)}) async-start(), calls=%async_computation.27 | async-start | bytes 3244032 | tf_op jit(solution)/shard_map/reduce_scatter | solution.py:357
  589.5 167.8 %reduce-scatter.33.cloned.1.call-start = ((), (), s32[]{:S(2)}) async-start(), calls=%async_computation.28 | async-start | bytes 3244032 | tf_op jit(solution)/shard_map/reduce_scatter | solution.py:358
  594.2 212.0 %reduce-scatter.35.cloned.1.call-start = ((), (), s32[]{:S(2)}) async-start(), calls=%async_computation.29 | async-start | bytes 3244032 | tf_op jit(solution)/shard_map/reduce_scatter | solution.py:359
  600.5 245.7 %reduce-scatter.29.cloned.1.call-start = ((), (), s32[]{:S(2)}) async-start(), calls=%async_computation.26 | async-start | bytes 1179648 | tf_op jit(solution)/shard_map/reduce_scatter | solution.py:356
  612.0 274.2 %reduce-scatter.23.cloned.1.call-start = ((), (), s32[]{:S(2)}) async-start(), calls=%async_computation.23 | async-start | bytes 1179648 | tf_op jit(solution)/shard_map/reduce_scatter | solution.py:353
  615.4 310.7 %reduce-scatter.21.cloned.1.call-start = ((), (), s32[]{:S(2)}) async-start(), calls=%async_computation.22 | async-start | bytes 1179648 | tf_op jit(solution)/shard_map/reduce_scatter | solution.py:352
  619.0 347.2 %reduce-scatter.25.cloned.1.call-start = ((), (), s32[]{:S(2)}) async-start(), calls=%async_computation.24 | async-start | bytes 1179648 | tf_op jit(solution)/shard_map/reduce_scatter | solution.py:354
  622.4 383.8 %reduce-scatter.27.cloned.1.call-start = ((), (), s32[]{:S(2)}) async-start(), calls=%async_computation.25 | async-start | bytes 1179648 | tf_op jit(solution)/shard_map/reduce_scatter | solution.py:355
  622.4 37.6 %copy-start.22 = (bf16[128,2,1024]{2,1,0:T(2,128)(2,1)S(1)}, bf16[128,2,1024]{2,1,0:T(2,128)(2,1)}, u32[]{:S(2)}) copy-start(bf16[128,2,1024]{2,1,0:T(2,128)(2,1)} %param.27) | copy-start | bytes 1572868
  (54 other events, 348.5 us)
Sparse Core Ops, SparseCore 0:
  10.8 48.6 all-gather.10
  132.7 81.2 reduce-scatter.12
  215.7 46.4 all-gather.18
  263.6 44.6 all-gather.12
  310.8 24.0 all-gather.14
  337.3 25.2 all-gather.16
  389.1 76.7 reduce-scatter.16
  469.5 46.4 all-gather.20
  572.9 41.6 reduce-scatter.18
  616.8 43.1 reduce-scatter.14
  664.0 44.2 reduce-scatter.30
  712.4 44.8 reduce-scatter.32
  761.3 44.9 reduce-scatter.34
  810.2 35.9 reduce-scatter.28
  850.1 36.0 reduce-scatter.22
  890.1 36.0 reduce-scatter.20
  930.1 35.9 reduce-scatter.24
  970.1 36.0 reduce-scatter.26
